TPU v7x, 256 devices: a whole 4x4x8 slice. The times are simulated.
256 devices in a mesh: dp: 8 (over z), expert: 8 (over x, core), tensor: 4 (over y).
Axes of the slice: x: 4, y: 4, z: 8, core: 2. Of those that a mesh axis runs over, the one named last changes fastest.
Arguments:
- skip_stream_entry: bfloat16 [4096, 4096], P(('dp', 'expert', 'tensor')), may hold values from -6 to 6
- question_vectors: bfloat16 [4096, 2048], P(('dp', 'expert'), 'tensor'), may hold values from -5 to 5
- fresh_lookup_vectors: bfloat16 [4096, 512], P(('dp', 'expert'), 'tensor'), may hold values from -5 to 5
- fresh_content_vectors: bfloat16 [4096, 512], P(('dp', 'expert'), 'tensor'), may hold values from -10 to 10
- stored_lookup_sheets: bfloat16 [2560, 4, 128, 128], P(('dp', 'expert'), 'tensor'), may hold values from -5 to 5
- stored_content_sheets: bfloat16 [2560, 4, 128, 128], P(('dp', 'expert'), 'tensor'), may hold values from -10 to 10
- sequence_sheet_map: int32 [1088, 8], P(('dp', 'expert')), may hold values from 0 to 39
- stored_position_counts: int32 [1088], P(('dp', 'expert')), may hold values from 2 to 1024
- attention_merge_matrix: bfloat16 [2048, 4096], P('tensor'), may hold values from -0.59765625 to 0.59765625
- premix_scale_factor: bfloat16 [4096], replicated, may hold values from 0.5 to 1.5
- chosen_specialists: int32 [4096, 2], P(('dp', 'expert', 'tensor')), may hold values from 0 to 7, all different within a row; in each aligned block of 16 rows (0 to 15, 16 to 31, ...) at most 6 rows name the same one
- selection_shares: float32 [4096, 2], P(('dp', 'expert', 'tensor')), may hold values from 0.2 to 1
- allowed_placements: int32 [8], replicated, may hold values from 2 to 3
- favored_specialist: int32 [1], replicated, may hold values from 0 to 7
- gating_matrices: bfloat16 [8, 7168, 4096], P('expert', ('dp', 'tensor')), may hold values from -0.09375 to 0.09375
- expand_matrices: bfloat16 [8, 7168, 4096], P('expert', ('dp', 'tensor')), may hold values from -0.09375 to 0.09375
- contract_matrices: bfloat16 [8, 7168, 4096], P('expert', ('dp', 'tensor')), may hold values from -0.0625 to 0.0625
Outputs:
- layer_out: bfloat16 [4096, 4096], P(('dp', 'expert', 'tensor'))
Inputs may be any that keep to these rules, and one draw needn't show every extreme that they name: `chosen_specialists`: in the 16 rows of one device no expert is named by more than 6 rows; a token names two different experts.
All inputs are finite; a program needn't handle non-finite values.
Results may differ from a plain program's by a relative error of at most 0.018.
Values may be sent and summed in bfloat16 or wider, within the bound.
A program may use at most 128 MiB of HBM per device.

v0:
```python
from functools import reduce
import math
import jax
import jax.numpy as jnp
from jax import lax
from jax.sharding import PartitionSpec as P

HD = 128
PLACEMENT_MOST = 6


def normalize(parts):
    highest = reduce(
        jnp.maximum,
        [
            jnp.max(jnp.where(visible, scores, -jnp.inf), axis=-1, keepdims=True)
            for scores, visible in parts
        ],
    )
    portions = [jnp.where(visible, jnp.exp(scores - highest), 0.0) for scores, visible in parts]
    denominator = reduce(
        jnp.add, [jnp.sum(portion, axis=-1, keepdims=True) for portion in portions]
    )
    return [(portion / denominator).astype(jnp.bfloat16) for portion in portions]


def attend(question_vectors, new_keys, new_values, key_pages, value_pages, table, spans):
    rows_all, head_count, head_width = question_vectors.shape
    kv_heads = new_keys.shape[1]
    group_size = head_count // kv_heads
    single_count = spans.shape[0] - 1
    page_count = table.shape[1]
    page_width = key_pages.shape[2]
    context = page_count * page_width
    inverse_root = 1.0 / math.sqrt(head_width)
    page_keys = key_pages[table]
    page_values = value_pages[table]
    grouped = question_vectors.reshape(rows_all, kv_heads, group_size, head_width)
    positions = jnp.arange(context, dtype=jnp.int32)
    single_q = grouped[:single_count]
    cache_dec = (
        jnp.einsum(
            "rkgh,rmkph->rkgmp",
            single_q,
            page_keys[:single_count],
            preferred_element_type=jnp.float32,
        ).reshape(single_count, kv_heads, group_size, context)
        * inverse_root
    )
    seen_dec = (positions[None, :] < spans[:single_count, None])[:, None, None, :]
    own_dec = (
        jnp.einsum(
            "rkgh,rkh->rkg", single_q, new_keys[:single_count], preferred_element_type=jnp.float32
        )[..., None]
        * inverse_root
    )
    weight_cache, weight_own = normalize(
        [(cache_dec, seen_dec), (own_dec, jnp.full(own_dec.shape, True))]
    )
    out_dec = jnp.einsum(
        "rkgmp,rmkph->rkgh",
        weight_cache.reshape(single_count, kv_heads, group_size, page_count, page_width),
        page_values[:single_count],
        preferred_element_type=jnp.float32,
    )
    out_dec = (
        out_dec
        + weight_own.astype(jnp.float32)
        * new_values[:single_count].astype(jnp.float32)[:, :, None, :]
    )
    prompt_q = grouped[single_count:]
    prompt_rows = rows_all - single_count
    cache_pro = (
        jnp.einsum(
            "rkgh,mkph->rkgmp",
            prompt_q,
            page_keys[single_count],
            preferred_element_type=jnp.float32,
        ).reshape(prompt_rows, kv_heads, group_size, context)
        * inverse_root
    )
    seen_pro = (positions < spans[single_count])[None, None, None, :]
    new_pro = (
        jnp.einsum(
            "rkgh,mkh->rkgm", prompt_q, new_keys[single_count:], preferred_element_type=jnp.float32
        )
        * inverse_root
    )
    prompt_index = jnp.arange(prompt_rows, dtype=jnp.int32)
    causal = (prompt_index[:, None] >= prompt_index[None, :])[:, None, None, :]
    weight_cpro, weight_npro = normalize([(cache_pro, seen_pro), (new_pro, causal)])
    out_pro = jnp.einsum(
        "rkgmp,mkph->rkgh",
        weight_cpro.reshape(prompt_rows, kv_heads, group_size, page_count, page_width),
        page_values[single_count],
        preferred_element_type=jnp.float32,
    )
    out_pro = out_pro + jnp.einsum(
        "rkgm,mkh->rkgh", weight_npro, new_values[single_count:], preferred_element_type=jnp.float32
    )
    joined = jnp.concatenate([out_dec, out_pro], axis=0).astype(jnp.bfloat16)
    return joined.reshape(rows_all, head_count * head_width)


def slot_table(member, ranking, keeping, slot_count):
    slot_hit = (
        ranking[:, :, None, None] == jnp.arange(slot_count, dtype=jnp.int32)[None, None, None, :]
    )
    return ((member[..., None] > 0) & keeping[:, :, None, None] & slot_hit).astype(jnp.bfloat16)


def expert_pass(send, gating_matrices, expand_matrices, contract_matrices):
    specialist_index, slot_count, model_width = send.shape
    holders = lax.axis_size("expert")
    local_count = gating_matrices.shape[0]
    arrived = lax.all_to_all(
        send.reshape(holders, local_count, slot_count, model_width),
        "expert",
        split_axis=0,
        concat_axis=0,
        tiled=True,
    )
    row_piece = lax.all_gather(arrived, ("dp", "tensor"), axis=0, tiled=True)
    gate_part = jnp.einsum(
        "qesd,efd->qesf", row_piece, gating_matrices, preferred_element_type=jnp.float32
    )
    up_part = jnp.einsum(
        "qesd,efd->qesf", row_piece, expand_matrices, preferred_element_type=jnp.float32
    )
    hidden = (jax.nn.silu(gate_part) * up_part).astype(jnp.bfloat16)
    partial_out = jnp.einsum(
        "qesf,efd->qesd", hidden, contract_matrices, preferred_element_type=jnp.float32
    ).astype(jnp.bfloat16)
    summed = lax.psum_scatter(
        lax.psum_scatter(partial_out, "dp", scatter_dimension=0, tiled=True),
        "tensor",
        scatter_dimension=0,
        tiled=True,
    )
    arrived_back = lax.all_to_all(summed, "expert", split_axis=0, concat_axis=0, tiled=True)
    return arrived_back.reshape(specialist_index, slot_count, model_width)


def local(
    skip_stream_entry,
    question_vectors,
    fresh_lookup_vectors,
    fresh_content_vectors,
    stored_lookup_sheets,
    stored_content_sheets,
    sequence_sheet_map,
    stored_position_counts,
    attention_merge_matrix,
    premix_scale_factor,
    chosen_specialists,
    selection_shares,
    allowed_placements,
    favored_specialist,
    gating_matrices,
    expand_matrices,
    contract_matrices,
):
    token_count = chosen_specialists.shape[0]
    specialist_index = allowed_placements.shape[0]
    picked = (
        chosen_specialists[:, :, None]
        == jnp.arange(specialist_index, dtype=jnp.int32)[None, None, :]
    ).astype(jnp.int32)
    flat_routes = picked.reshape(token_count * 2, specialist_index)
    busiest_specialist = favored_specialist[0]
    before = (jnp.cumsum(flat_routes, axis=0) - flat_routes).reshape(
        token_count, 2, specialist_index
    )
    ranking = jnp.sum(before * picked, axis=2)
    placement_ceiling = jnp.where(
        jnp.arange(specialist_index, dtype=jnp.int32) == busiest_specialist,
        PLACEMENT_MOST,
        allowed_placements,
    )
    keeping = ranking < jnp.sum(picked * placement_ceiling[None, None, :], axis=2)
    row_total = question_vectors.shape[0]
    heads_out = attend(
        question_vectors.reshape(row_total, -1, HD),
        fresh_lookup_vectors.reshape(row_total, -1, HD),
        fresh_content_vectors.reshape(row_total, -1, HD),
        stored_lookup_sheets,
        stored_content_sheets,
        sequence_sheet_map,
        stored_position_counts,
    )
    own_attn = lax.psum_scatter(
        jnp.dot(heads_out, attention_merge_matrix, preferred_element_type=jnp.float32).astype(
            jnp.bfloat16
        ),
        "tensor",
        scatter_dimension=0,
        tiled=True,
    ).astype(jnp.float32)
    stream = (skip_stream_entry.astype(jnp.float32) + own_attn).astype(jnp.bfloat16)
    wide = stream.astype(jnp.float32)
    squares = jnp.mean(wide * wide, axis=1, keepdims=True)
    normed = (wide * lax.rsqrt(squares + 1e-05) * premix_scale_factor.astype(jnp.float32)).astype(
        jnp.bfloat16
    )
    main_slots = PLACEMENT_MOST
    table_main = slot_table(picked, ranking, keeping, main_slots)
    send = jnp.einsum(
        "nkes,nd->esd", table_main, normed, preferred_element_type=jnp.float32
    ).astype(jnp.bfloat16)
    expert_out = expert_pass(send, gating_matrices, expand_matrices, contract_matrices)
    chosen = jnp.einsum("nkes,esd->nkd", table_main, expert_out, preferred_element_type=jnp.float32)
    mixed = jnp.sum(selection_shares[:, :, None] * chosen, axis=1)
    return (wide + mixed).astype(jnp.bfloat16)


def solution(mesh):
    placed = (
        P(("dp", "expert", "tensor"), None),
        P(("dp", "expert"), "tensor"),
        P(("dp", "expert"), "tensor"),
        P(("dp", "expert"), "tensor"),
        P(("dp", "expert"), "tensor", None, None),
        P(("dp", "expert"), "tensor", None, None),
        P(("dp", "expert"), None),
        P(("dp", "expert")),
        P("tensor", None),
        P(),
        P(("dp", "expert", "tensor"), None),
        P(("dp", "expert", "tensor"), None),
        P(),
        P(),
        P("expert", ("dp", "tensor"), None),
        P("expert", ("dp", "tensor"), None),
        P("expert", ("dp", "tensor"), None),
    )
    return jax.shard_map(
        local,
        mesh=mesh,
        in_specs=placed,
        out_specs=P(("dp", "expert", "tensor"), None),
        check_vma=False,
    )
```

profile of v0, /device:TPU:1, one launch (start us, length us, event | category | flops | bytes accessed | tf_op | source)
XLA Modules:
  0.0 416.9 jit_solution(13904441723688626765)
XLA Ops:
  7.4 1.2 slice.49
  8.7 1.2 broadcast_compare_fusion.1
  10.5 1.3 slice_bitcast_fusion.5
  12.0 1.3 slice_convert_fusion
  13.3 1.6 select_reduce_fusion.2
  14.8 8.8 %gather_fusion.1 = bf16[136,128,128]{2,1,0:T(8,128)(2,1)} fusion(bf16[40,128,128]{2,1,0:T(8,128)(2,1)} %bitcast.219, s32[1024]{0:T(1024)S(1)} %pad_clamp_fusion), kind=kCustom, calls=%fused_computation.1 | custom fusion | bytes 8913440 | tf_op jit(solution)/shard_map/gather | solution.py:37
  23.7 1.3 copy-done.1
  25.0 7.5 %gather_fusion = bf16[136,128,128]{2,1,0:T(8,128)(2,1)} fusion(bf16[40,128,128]{2,1,0:T(8,128)(2,1)S(1)} %bitcast.220, s32[1024]{0:T(1024)S(1)} %pad_clamp_fusion), kind=kCustom, calls=%fused_computation | custom fusion | bytes 8913440 | tf_op jit(solution)/shard_map/gather | solution.py:36
  33.4 1.7 select_reduce_fusion
  36.4 1.3 select_reduce_fusion.1
  38.0 1.4 slice-done.2
  40.1 1.6 convolution_convert_fusion
  43.4 24.8 %reduce-scatter.6.cloned.1.call-done = bf16[16,4096]{1,0:T(8,128)(2,1)} async-done(((bf16[64,4096]{1,0:T(8,128)(2,1)}), bf16[16,4096]{1,0:T(8,128)(2,1)}) %reduce-scatter.6.cloned.1.call-update) | async-done | bytes 131088 | tf_op jit(solution)/shard_map/reduce_scatter | solution.py:191
  68.1 1.1 fusion.53
  69.2 1.2 fusion.5
  70.6 15.7 %all_to_all.10 = bf16[8,1,6,4096]{3,2,1,0:T(8,128)(2,1)S(1)} all-to-all(bf16[8,1,6,4096]{3,2,1,0:T(8,128)(2,1)S(1)} %copy.41), channel_id=1, replica_groups=mesh['dp'=8,'expert'=8,'tensor'=4] {'expert'}, dimensions={0} | all-to-all | bytes 786432 | tf_op jit(solution)/shard_map/all_to_all | solution.py:116
  87.6 117.5 %all-gather.2.cloned.1.call-done = bf16[256,1,6,4096]{3,0,2,1:T(8,128)(2,1)} async-done(((bf16[8,1,6,4096]{3,0,2,1:T(8,128)(2,1)}), bf16[256,1,6,4096]{3,0,2,1:T(8,128)(2,1)}) %all-gather.2.cloned.1.call-update) | async-done | bytes 12582928 | tf_op jit(solution)/shard_map/all_gather | solution.py:123
  205.1 7.5 %fusion.9 = f32[256,1,6,224]{0,3,2,1:T(8,128)S(1)} fusion(bf16[1,224,4096]{2,1,0:T(8,128)(2,1)} %param.31, bf16[256,1,6,4096]{3,0,2,1:T(8,128)(2,1)} %all-gather.2.cloned.1.call-done), kind=kOutput, calls=%fused_computation.15 | convolution fusion | flops 2818572288 | bytes 15794176 | tf_op jit(solution)/shard_map/qesd,efd->qesf/dot_general | solution.py:124
  212.6 19.3 %convert_bitcast_fusion = bf16[256,1,6,4096]{3,0,2,1:T(8,128)(2,1)} fusion(bf16[1,224,4096]{2,1,0:T(8,128)(2,1)S(1)} %copy-done, bf16[1,224,4096]{2,1,0:T(8,128)(2,1)} %param.32, bf16[256,1,6,4096]{3,0,2,1:T(8,128)(2,1)} %all-gather.2.cloned.1.call-done, f32[256,1,6,224]{0,3,2,1:T(8,128)S(1)} %fusion.9), kind=kOutput, calls=%fused_computation.6 | convolution fusion | flops 5645500416 | bytes 30212096 | tf_op jit(solution)/shard_map/qesf,efd->qesd/dot_general | solution.py:131
  232.0 132.1 %reduce-scatter.8.cloned.1.call-done = bf16[32,1,6,4096]{3,0,2,1:T(8,128)(2,1)} async-done(((bf16[256,1,6,4096]{3,0,2,1:T(8,128)(2,1)}), bf16[32,1,6,4096]{3,0,2,1:T(8,128)(2,1)}) %reduce-scatter.8.cloned.1.call-update) | async-done | bytes 1572880 | tf_op jit(solution)/shard_map/reduce_scatter | solution.py:135
  364.1 2.7 copy.58
  366.8 26.2 %reduce-scatter.10.cloned.1.call-done = bf16[8,24576]{1,0:T(8,128)(2,1)} async-done(((bf16[32,24576]{1,0:T(8,128)(2,1)}), bf16[8,24576]{1,0:T(8,128)(2,1)}) %reduce-scatter.10.cloned.1.call-update) | async-done | bytes 393232
  393.0 1.2 copy.43
  394.2 15.1 %all_to_all.11 = bf16[8,1,6,4096]{3,2,1,0:T(8,128)(2,1)S(1)} all-to-all(bf16[8,1,6,4096]{3,2,1,0:T(8,128)(2,1)S(1)} %copy.43), channel_id=1, replica_groups=mesh['dp'=8,'expert'=8,'tensor'=4] {'expert'}, dimensions={0} | all-to-all | bytes 786432 | tf_op jit(solution)/shard_map/all_to_all | solution.py:140
  (90 shorter events, 8.3 us)
Async XLA Ops:
  6.5 206.1 %copy-start = (bf16[1,224,4096]{2,1,0:T(8,128)(2,1)S(1)}, bf16[1,224,4096]{2,1,0:T(8,128)(2,1)}, u32[]{:S(2)}) copy-start(bf16[1,224,4096]{2,1,0:T(8,128)(2,1)} %param.33) | copy-start | bytes 5505028
  6.5 61.6 %reduce-scatter.6.cloned.1.call-start = ((), (), s32[]{:S(2)}) async-start(), calls=%async_computation.5 | async-start | bytes 655360 | tf_op jit(solution)/shard_map/reduce_scatter | solution.py:191
  23.7 1.3 copy-start.1
  25.0 10.7 %slice-start = ((s8[4456448]{0:T(1024)(128)(4,1)}), s8[262144]{0:T(1024)(128)(4,1)S(1)}, s32[]{:S(2)}) async-start(s8[4456448]{0:T(1024)(128)(4,1)} %bitcast.215), calls=%async_computation.9 | async-start | bytes 524288
  32.5 0.8 copy-start.8
  32.5 0.8 copy-start.12
  32.6 2.6 copy-start.10
  32.6 2.9 copy-start.13
  32.6 3.1 slice-start.1
  33.4 2.7 copy-start.14
  33.4 2.8 copy-start.9
  33.4 3.0 slice-start.3
  35.7 3.6 slice-start.2
  35.7 3.6 copy-start.7
  36.4 3.8 copy-start.2
  39.3 2.5 copy-start.5
  39.3 3.8 copy-start.6
  39.3 3.8 copy-start.15
  39.4 28.8 %copy-start.3 = (bf16[16,4096]{1,0:T(8,128)(2,1)S(1)}, bf16[16,4096]{1,0:T(8,128)(2,1)}, u32[]{:S(2)}) copy-start(bf16[16,4096]{1,0:T(8,128)(2,1)} %param.17) | copy-start | bytes 393220
  41.8 163.3 %all-gather.2.cloned.1.call-start = ((), (), s32[]{:S(2)}) async-start(), calls=%async_computation.6 | async-start | bytes 12976128 | tf_op jit(solution)/shard_map/all_gather | solution.py:123
  87.4 276.7 %reduce-scatter.8.cloned.1.call-start = ((), (), s32[]{:S(2)}) async-start(), calls=%async_computation.7 | async-start | bytes 14155776 | tf_op jit(solution)/shard_map/reduce_scatter | solution.py:135
  231.9 177.3 %copy-start.11 = (f32[16,2]{0,1:T(2,128)S(1)}, f32[16,2]{0,1:T(2,128)}, u32[]{:S(2)}) copy-start(f32[16,2]{0,1:T(2,128)} %param.28) | copy-start | bytes 388
  231.9 177.7 %copy-start.4 = (bf16[16,4096]{1,0:T(8,128)(2,1)S(1)}, bf16[16,4096]{1,0:T(8,128)(2,1)}, u32[]{:S(2)}) copy-start(bf16[16,4096]{1,0:T(8,128)(2,1)} %reduce-scatter.6.cloned.1.call-done) | copy-start | bytes 393220
  231.9 161.0 %reduce-scatter.10.cloned.1.call-start = ((), (), s32[]{:S(2)}) async-start(), calls=%async_computation.8 | async-start | bytes 1966080
Sparse Core Ops, SparseCore 0:
  41.9 26.1 reduce-scatter.5
  87.5 117.5 all-gather.1
  232.0 131.9 reduce-scatter.7
  366.9 26.0 reduce-scatter.9
where the time goes:
time: 417 us
  waiting for transfers between devices  301 us (72%)
  matrix products  35.9 us (9%)
  blocking collectives  30.8 us (7%)
  local copies, waits for them, and re-layouts  29 us (7%)
  between operations  14.2 us (3%)
  other arithmetic  6.11 us (1%)
    reduce_scatter x1, waiting for transfers between devices, expert_pass(): lax.psum_scatter(partial_out, 'dp', scatter_dimension=0, tiled=True)  132 us
    all_gather x1, waiting for transfers between devices, expert_pass(): row_piece = lax.all_gather(arrived, ('dp', 'tensor'), axis=0, tiled=True)  118 us
    unnamed x5, waiting for transfers between devices  26.2 us
    reduce_scatter x1, waiting for transfers between devices, local(): lax.psum_scatter(jnp.dot(heads_out, attention_merge_matrix, preferred_ele...  24.8 us
    dot_general x1, matrix products, expert_pass(): jnp.einsum('qesf,efd->qesd', hidden, contract_matrices, preferred_element...  19.3 us
    all_to_all x1, blocking collectives, expert_pass(): lax.all_to_all(send.reshape(holders, local_count, slot_count, model_width...  15.7 us
    all_to_all x1, blocking collectives, expert_pass(): lax.all_to_all(summed, 'expert', split_axis=0, concat_axis=0, tiled=True)  15.1 us
    gather x1, local copies, waits for them, and re-layouts, attend(): page_values = value_pages[table]  8.83 us
  transfers between devices with their start and end apart: 4, of which 4 were waited for; matrix products, arithmetic and copies ran while one was open for 0% of the time, Pallas kernels for 0%

commit v1 on v0

--- a/solution.py
+++ b/solution.py
@@ -120,7 +120,8 @@
         concat_axis=0,
         tiled=True,
     )
-    row_piece = lax.all_gather(arrived, ("dp", "tensor"), axis=0, tiled=True)
+    repeated = jnp.stack([arrived] * lax.axis_size(("dp", "tensor")))
+    row_piece = jnp.concatenate(lax.all_to_all(repeated, ("dp", "tensor"), 0, 0), axis=0)
     gate_part = jnp.einsum(
         "qesd,efd->qesf", row_piece, gating_matrices, preferred_element_type=jnp.float32
     )

time: 417 us -> 587 us (1.41)
  blocking collectives: 30.8 us -> 312 us
  waiting for transfers between devices: 301 us -> 183 us
  local copies, waits for them, and re-layouts: 29 us -> 38.9 us
    all_to_all x0 -> x1, blocking collectives: none -> 281 us  [expert_pass(): lax.all_to_all(repeated, ('dp', 'tensor'), 0, 0)]
    all_gather x1 -> x0, waiting for transfers between devices: 118 us -> none  [expert_pass(): row_piece = lax.all_gather(arrived, ('dp', 'tensor'), axis=0, tiled=True)]
    another operation x2 -> x3, local copies, waits for them, and re-layouts: 0.03 us -> 6.18 us  [the longest x1 6.16 us: expert_pass(): repeated = jnp.stack([arrived] * lax.axis_size(('dp', 'tensor')))]
    unnamed x5 -> x4, waiting for transfers between devices: 26.2 us -> 26.2 us
  transfers between devices with their start and end apart: 4 -> 3, of which waited for: 4 -> 3; matrix products, arithmetic and copies ran while one was open for 0% -> 0% of each run, Pallas kernels for 0% -> 0%
where the time goes in v1:
time: 587 us
  blocking collectives  312 us (53%)
  waiting for transfers between devices  183 us (31%)
  local copies, waits for them, and re-layouts  38.9 us (7%)
  matrix products  32.4 us (6%)
  between operations  14.1 us (2%)
  other arithmetic  6.11 us (1%)
    all_to_all x1, blocking collectives, expert_pass(): lax.all_to_all(repeated, ('dp', 'tensor'), 0, 0)  281 us
    reduce_scatter x1, waiting for transfers between devices, expert_pass(): lax.psum_scatter(partial_out, 'dp', scatter_dimension=0, tiled=True)  132 us
    unnamed x4, waiting for transfers between devices  26.2 us
    reduce_scatter x1, waiting for transfers between devices, local(): lax.psum_scatter(jnp.dot(heads_out, attention_merge_matrix, preferred_ele...  24.8 us
    dot_general x1, matrix products, expert_pass(): jnp.einsum('qesf,efd->qesd', hidden, contract_matrices, preferred_element...  19.4 us
    all_to_all x1, blocking collectives, expert_pass(): lax.all_to_all(send.reshape(holders, local_count, slot_count, model_width...  15.7 us
    all_to_all x1, blocking collectives, expert_pass(): lax.all_to_all(summed, 'expert', split_axis=0, concat_axis=0, tiled=True)  15 us
  transfers between devices with their start and end apart: 3, of which 3 were waited for; matrix products, arithmetic and copies ran while one was open for 0% of the time, Pallas kernels for 0%

profile of v1, /device:TPU:1, one launch (start us, length us, event | category | flops | bytes accessed | tf_op | source)
XLA Modules:
  0.0 586.9 jit_solution(1557035913576616416)
XLA Ops:
  7.4 1.2 slice.49
  10.5 1.3 slice_bitcast_fusion.5
  12.0 1.3 slice_convert_fusion
  13.3 1.6 select_reduce_fusion.2
  14.8 8.8 %gather_fusion.1 = bf16[136,128,128]{2,1,0:T(8,128)(2,1)} fusion(bf16[40,128,128]{2,1,0:T(8,128)(2,1)} %bitcast.220, s32[1024]{0:T(1024)S(1)} %pad_clamp_fusion), kind=kCustom, calls=%fused_computation.1 | custom fusion | bytes 8913440 | tf_op jit(solution)/shard_map/gather | solution.py:37
  23.7 1.3 copy-done.1
  25.0 7.5 %gather_fusion = bf16[136,128,128]{2,1,0:T(8,128)(2,1)} fusion(bf16[40,128,128]{2,1,0:T(8,128)(2,1)S(1)} %bitcast.221, s32[1024]{0:T(1024)S(1)} %pad_clamp_fusion), kind=kCustom, calls=%fused_computation | custom fusion | bytes 8913440 | tf_op jit(solution)/shard_map/gather | solution.py:36
  33.4 1.7 select_reduce_fusion
  36.4 1.3 select_reduce_fusion.1
  38.0 1.4 slice-done.2
  40.1 1.6 convolution_convert_fusion
  43.4 24.8 %reduce-scatter.6.cloned.1.call-done = bf16[16,4096]{1,0:T(8,128)(2,1)} async-done(((bf16[64,4096]{1,0:T(8,128)(2,1)}), bf16[16,4096]{1,0:T(8,128)(2,1)}) %reduce-scatter.6.cloned.1.call-update) | async-done | bytes 131088 | tf_op jit(solution)/shard_map/reduce_scatter | solution.py:192
  69.2 1.2 fusion.7
  70.6 15.7 %all_to_all.18 = bf16[8,1,6,4096]{3,2,1,0:T(8,128)(2,1)S(1)} all-to-all(bf16[8,1,6,4096]{3,2,1,0:T(8,128)(2,1)S(1)} %copy.41), channel_id=1, replica_groups=mesh['dp'=8,'expert'=8,'tensor'=4] {'expert'}, dimensions={0} | all-to-all | bytes 786432 | tf_op jit(solution)/shard_map/all_to_all | solution.py:116
  86.6 6.2 %stack.2 = bf16[32,8,1,6,4096]{4,1,3,2,0:T(8,128)(2,1)} broadcast(bf16[8,6,4096]{2,0,1:T(8,128)(2,1)S(1)} %copy.42), dimensions={1,3,4} | broadcast | bytes 12976128 | tf_op jit(solution)/shard_map/stack | solution.py:123
  92.8 281.1 %all_to_all.19 = bf16[32,8,1,6,4096]{4,1,3,2,0:T(8,128)(2,1)S(1)} all-to-all(bf16[32,8,1,6,4096]{4,1,3,2,0:T(8,128)(2,1)} %stack.2), channel_id=1, replica_groups=mesh['dp'=8,'expert'=8,'tensor'=4] {'dp','tensor'}, dimensions={0} | all-to-all | bytes 25165824 | tf_op jit(solution)/shard_map/all_to_all | solution.py:124
  373.8 4.5 copy-done.2
  378.3 3.8 fusion.11
  382.1 19.4 %convert_bitcast_fusion = bf16[256,1,6,4096]{3,0,2,1:T(8,128)(2,1)} fusion(bf16[1,224,4096]{2,1,0:T(8,128)(2,1)S(1)} %copy-done, bf16[1,224,4096]{2,1,0:T(8,128)(2,1)} %param.32, bf16[32,8,1,6,4096]{4,1,3,2,0:T(8,128)(2,1)} %copy-done.2, f32[256,1,6,224]{0,3,2,1:T(8,128)S(1)} %fusion.11), kind=kOutput, calls=%fused_computation.6 | convolution fusion | flops 5645500416 | bytes 30212096 | tf_op jit(solution)/shard_map/qesf,efd->qesd/dot_general | solution.py:132
  401.7 132.5 %reduce-scatter.8.cloned.1.call-done = bf16[32,1,6,4096]{3,0,2,1:T(8,128)(2,1)} async-done(((bf16[256,1,6,4096]{3,0,2,1:T(8,128)(2,1)}), bf16[32,1,6,4096]{3,0,2,1:T(8,128)(2,1)}) %reduce-scatter.8.cloned.1.call-update) | async-done | bytes 1572880 | tf_op jit(solution)/shard_map/reduce_scatter | solution.py:136
  534.1 2.7 copy.59
  536.8 26.1 %reduce-scatter.10.cloned.1.call-done = bf16[8,24576]{1,0:T(8,128)(2,1)} async-done(((bf16[32,24576]{1,0:T(8,128)(2,1)}), bf16[8,24576]{1,0:T(8,128)(2,1)}) %reduce-scatter.10.cloned.1.call-update) | async-done | bytes 393232
  563.0 1.2 copy.44
  564.2 15.0 %all_to_all.20 = bf16[8,1,6,4096]{3,2,1,0:T(8,128)(2,1)S(1)} all-to-all(bf16[8,1,6,4096]{3,2,1,0:T(8,128)(2,1)S(1)} %copy.44), channel_id=1, replica_groups=mesh['dp'=8,'expert'=8,'tensor'=4] {'expert'}, dimensions={0} | all-to-all | bytes 786432 | tf_op jit(solution)/shard_map/all_to_all | solution.py:141
  (93 shorter events, 9.5 us)
Async XLA Ops:
  6.5 375.6 %copy-start = (bf16[1,224,4096]{2,1,0:T(8,128)(2,1)S(1)}, bf16[1,224,4096]{2,1,0:T(8,128)(2,1)}, u32[]{:S(2)}) copy-start(bf16[1,224,4096]{2,1,0:T(8,128)(2,1)} %param.33) | copy-start | bytes 5505028
  6.5 61.6 %reduce-scatter.6.cloned.1.call-start = ((), (), s32[]{:S(2)}) async-start(), calls=%async_computation.6 | async-start | bytes 655360 | tf_op jit(solution)/shard_map/reduce_scatter | solution.py:192
  23.7 1.3 copy-start.1
  25.0 10.7 %slice-start = ((s8[4456448]{0:T(1024)(128)(4,1)}), s8[262144]{0:T(1024)(128)(4,1)S(1)}, s32[]{:S(2)}) async-start(s8[4456448]{0:T(1024)(128)(4,1)} %bitcast.216), calls=%async_computation.9 | async-start | bytes 524288
  32.5 0.8 copy-start.9
  32.6 2.6 copy-start.11
  32.6 2.9 copy-start.14
  32.6 3.1 slice-start.1
  33.4 2.7 copy-start.15
  33.4 2.8 copy-start.10
  33.4 3.0 slice-start.3
  35.7 3.6 slice-start.2
  35.7 3.6 copy-start.8
  36.4 3.8 copy-start.3
  39.3 2.5 copy-start.6
  39.3 3.8 copy-start.7
  39.3 3.8 copy-start.17
  39.4 28.8 %copy-start.4 = (bf16[16,4096]{1,0:T(8,128)(2,1)S(1)}, bf16[16,4096]{1,0:T(8,128)(2,1)}, u32[]{:S(2)}) copy-start(bf16[16,4096]{1,0:T(8,128)(2,1)} %param.17) | copy-start | bytes 393220
  41.8 492.3 %reduce-scatter.8.cloned.1.call-start = ((), (), s32[]{:S(2)}) async-start(), calls=%async_computation.7 | async-start | bytes 14155776 | tf_op jit(solution)/shard_map/reduce_scatter | solution.py:136
  92.8 285.5 %copy-start.16 = (bf16[1,224,4096]{2,1,0:T(8,128)(2,1)S(1)}, bf16[1,224,4096]{2,1,0:T(8,128)(2,1)}, u32[]{:S(2)}) copy-start(bf16[1,224,4096]{2,1,0:T(8,128)(2,1)} %param.31) | copy-start | bytes 5505028
  373.8 4.5 copy-start.2
  401.6 177.7 %copy-start.12 = (f32[16,2]{0,1:T(2,128)S(1)}, f32[16,2]{0,1:T(2,128)}, u32[]{:S(2)}) copy-start(f32[16,2]{0,1:T(2,128)} %param.28) | copy-start | bytes 388
  401.6 178.0 %copy-start.5 = (bf16[16,4096]{1,0:T(8,128)(2,1)S(1)}, bf16[16,4096]{1,0:T(8,128)(2,1)}, u32[]{:S(2)}) copy-start(bf16[16,4096]{1,0:T(8,128)(2,1)} %reduce-scatter.6.cloned.1.call-done) | copy-start | bytes 393220
  401.6 161.4 %reduce-scatter.10.cloned.1.call-start = ((), (), s32[]{:S(2)}) async-start(), calls=%async_computation.8 | async-start | bytes 1966080
  (1 other events, 0.8 us)
Sparse Core Ops, SparseCore 0:
  41.9 26.1 reduce-scatter.5
  401.7 132.3 reduce-scatter.7
  537.0 25.9 reduce-scatter.9
